TPU v7x, 32 devices: a whole 2x2x4 slice. The times are simulated.
32 devices in a mesh: sample: 4 (over x, core), space: 8 (over z, y).
Axes of the slice: x: 2, y: 2, z: 4, core: 2. Of those that a mesh axis runs over, the one named last changes fastest.
Arguments:
- acts: bfloat16 [8, 8, 16, 8, 8, 128], P('sample', 'space'), may hold values from -6 to 6
- weight: float32 [3456, 128], P('space'), may hold values from -0.109375 to 0.109375
- moment: float32 [3456, 128], P('space'), may hold values from -3 to 3
- second: float32 [3456, 128], P('space'), may hold values from 0.05 to 2
- cotangent: bfloat16 [8, 8, 16, 8, 8, 128], P('sample', 'space'), may hold values from -6 to 6
Outputs:
- output: bfloat16 [8, 8, 16, 8, 8, 128], P('sample', 'space')
- input_grad: bfloat16 [8, 8, 16, 8, 8, 128], P('sample', 'space')
- weight_grad: float32 [3456, 128], P('space')
- new_weight: float32 [3456, 128], P('space')
- new_moment: float32 [3456, 128], P('space')
- new_second: float32 [3456, 128], P('space')
All inputs are finite; a program needn't handle non-finite values.
Results may differ from a plain program's by a relative error of at most 0.0062.
Values may be sent and summed in bfloat16 or wider, within the bound.
A program may use at most 64 MiB of HBM per device.

v0:
```python
import jax
import jax.numpy as jnp
from jax import lax
from jax.sharding import PartitionSpec as P

GY = 2
GZ = 4
root_coef = 0.7978845608
cubic_coef = 0.044715


def shifted(value, axis, by):
    devices = lax.axis_size(axis)
    pairs = [(i, i + by) for i in range(devices) if 0 <= i + by < devices]
    return lax.ppermute(value, axis, pairs)


def convolve(field, kernel):
    return lax.conv_general_dilated(
        field,
        kernel,
        (1, 1, 1),
        "VALID",
        dimension_numbers=("NDHWC", "DHWIO", "NDHWC"),
        preferred_element_type=jnp.float32,
    )


def activate(pre):
    inner = root_coef * (pre + cubic_coef * pre * pre * pre)
    tval = jnp.tanh(inner)
    value = 0.5 * pre * (1.0 + tval)
    slope = 0.5 * (1.0 + tval) + 0.5 * pre * (1.0 - tval * tval) * root_coef * (
        1.0 + 3.0 * cubic_coef * pre * pre
    )
    return (value, slope)


def extend(field):
    place = lax.axis_index("space")
    groups = lax.axis_size("space") // (GY * GZ)
    coord_z = place % GZ
    coord_y = place // GZ % GY
    coord_x = place // (GZ * GY)
    for dim, stride, coord, count in (
        (3, 1, coord_z, GZ),
        (2, GZ, coord_y, GY),
        (1, GY * GZ, coord_x, groups),
    ):
        length = field.shape[dim]
        first_layer = lax.slice_in_dim(field, 0, 1, 1, dim)
        last_layer = lax.slice_in_dim(field, length - 1, length, 1, dim)
        below = shifted(last_layer, "space", stride)
        above = shifted(first_layer, "space", -stride)
        below = jnp.where(coord > 0, below, jnp.zeros_like(below))
        above = jnp.where(coord < count - 1, above, jnp.zeros_like(above))
        field = jnp.concatenate([below, field, above], dim)
    return field


def kernel_terms(padded, grad_pre):
    nx, ny, nz = (grad_pre.shape[1], grad_pre.shape[2], grad_pre.shape[3])
    terms = []
    for kx in range(3):
        for ky in range(3):
            for kz in range(3):
                window = padded[:, kx : kx + nx, ky : ky + ny, kz : kz + nz, :]
                terms.append(
                    lax.dot_general(
                        window,
                        grad_pre,
                        (((0, 1, 2, 3), (0, 1, 2, 3)), ((), ())),
                        preferred_element_type=jnp.float32,
                    )
                )
    stacked = jnp.stack(terms, 0)
    return stacked.reshape(27 * stacked.shape[1], stacked.shape[2])


def local(acts, weight, moment, second, cotangent):
    field = acts[:, 0]
    grad_out = cotangent[:, 0]
    channels = weight.shape[1]
    rows_bf = weight.astype(jnp.bfloat16)
    whole = lax.all_gather(rows_bf, "space", axis=0, tiled=True)
    kernel = whole.reshape(3, 3, 3, channels, channels)
    padded = extend(field)
    pre = convolve(padded, kernel)
    value, slope = activate(pre)
    output = value.astype(jnp.bfloat16)
    grad_pre = (grad_out.astype(jnp.float32) * slope).astype(jnp.bfloat16)
    flipped = jnp.flip(kernel, (0, 1, 2)).transpose(0, 1, 2, 4, 3)
    grad_padded = extend(grad_pre)
    input_grad = convolve(grad_padded, flipped).astype(jnp.bfloat16)
    total = (
        field.shape[0]
        * lax.axis_size("sample")
        * lax.axis_size("space")
        * field.shape[1]
        * field.shape[2]
        * field.shape[3]
    )
    local_terms = kernel_terms(padded, grad_pre) * float(total) ** (-0.5)
    owned = lax.psum_scatter(local_terms, "space", scatter_dimension=0, tiled=True)
    weight_grad = lax.psum(owned, "sample")
    new_moment = 0.9 * moment + 0.1 * weight_grad
    new_second = 0.999 * second + 0.001 * weight_grad * weight_grad
    first_fix = 1.0 - 0.9**10
    second_fix = 1.0 - 0.999**10
    new_weight = weight - 0.001 * (new_moment / first_fix) / (
        jnp.sqrt(new_second / second_fix) + 1e-08
    )
    return (output[:, None], input_grad[:, None], weight_grad, new_weight, new_moment, new_second)


def solution(mesh):
    in_specs = (
        P("sample", "space", None, None, None, None),
        P("space", None),
        P("space", None),
        P("space", None),
        P("sample", "space", None, None, None, None),
    )
    out_specs = (
        P("sample", "space", None, None, None, None),
        P("sample", "space", None, None, None, None),
        P("space", None),
        P("space", None),
        P("space", None),
        P("space", None),
    )
    return jax.shard_map(local, mesh=mesh, in_specs=in_specs, out_specs=out_specs, check_vma=False)
```

profile of v0, /device:TPU:0, one launch (start us, length us, event | category | flops | bytes accessed | tf_op | source)
XLA Modules:
  0.0 203.3 jit_solution(16130695142617238557)
XLA Ops:
  7.2 1.5 fusion.71
  8.7 1.3 collective-permute-start.1
  10.0 5.5 %collective-permute-start = (bf16[2,16,8,1,128]{4,3,2,1,0:T(2,128)(2,1)S(1)}, bf16[2,16,8,1,128]{4,3,2,1,0:T(2,128)(2,1)S(1)}, u32[]{:S(2)}, u32[]{:S(2)}) collective-permute-start(bf16[2,16,8,1,128]{4,3,2,1,0:T(2,128)(2,1)S(1)} %get-tuple-element.37), channel_id=1, source_target_pairs={{0,1},{1,2},{2,3},{3,4},{4,5},{5,6},{6,7},{8,9},{9,10},{10,11},{11... | collective-permute-start | bytes 196616 | tf_op jit(solution)/shard_map/ppermute | solution.py:15
  15.5 1.0 convert_element_type.18
  16.5 0.6 collective-permute-done.1
  17.2 2.8 %collective-permute-done = bf16[2,16,8,1,128]{4,3,2,1,0:T(2,128)(2,1)S(1)} collective-permute-done((bf16[2,16,8,1,128]{4,3,2,1,0:T(2,128)(2,1)S(1)}, bf16[2,16,8,1,128]{4,3,2,1,0:T(2,128)(2,1)S(1)}, u32[]{:S(2)}, u32[]{:S(2)}) %collective-permute-start) | collective-permute-done | bytes 65568 | tf_op jit(solution)/shard_map/ppermute | solution.py:15
  20.2 0.2 pad_maximum_fusion.13
  20.4 1.3 collective-permute-start.3
  21.7 35.9 %all_gather.3 = bf16[3456,128]{1,0:T(8,128)(2,1)S(1)} all-gather(bf16[432,128]{1,0:T(8,128)(2,1)S(1)} %convert_element_type.18), channel_id=1, replica_groups=mesh['sample'=4,'space'=8] {'space'}, dimensions={0}, use_global_device_ids=true | all-gather | bytes 995328 | tf_op jit(solution)/shard_map/all_gather | solution.py:85
  57.6 1.3 collective-permute-start.2
  58.9 2.5 %collective-permute-done.2 = bf16[2,16,1,10,128]{4,3,2,1,0:T(8,128)(2,1)S(1)} collective-permute-done((bf16[2,16,1,10,128]{4,3,2,1,0:T(8,128)(2,1)S(1)}, bf16[2,16,1,10,128]{4,3,2,1,0:T(8,128)(2,1)S(1)}, u32[]{:S(2)}, u32[]{:S(2)}) %collective-permute-start.2) | collective-permute-done | bytes 81952 | tf_op jit(solution)/shard_map/ppermute | solution.py:15
  61.5 0.7 collective-permute-start.5
  62.1 1.4 pad_maximum_fusion.3
  63.5 0.7 collective-permute-start.4
  64.2 0.7 pad_maximum_fusion
  65.0 1.5 pad_maximum_fusion.2
  66.6 6.3 %fusion.36 = f32[2,16,8,8,128]{4,0,3,2,1:T(2,128)S(1)} fusion(bf16[3,3,3,128,128]{4,3,2,1,0:T(8,128)(2,1)S(1)} %bitcast.272, bf16[2,18,10,10,128]{4,3,2,1,0:T(8,128)(2,1)S(1)} %pad_maximum_fusion), kind=kOutput, calls=%fused_computation.73 | convolution fusion | flops 1811939328 | bytes 2854912 | tf_op jit(solution)/shard_map/conv_general_dilated | solution.py:19
  72.9 1.6 fusion.34
  74.4 0.3 fusion.27
  74.8 0.4 fusion.26
  75.2 0.4 fusion.25
  75.5 0.3 fusion.24
  75.9 0.4 fusion.23
  76.3 0.4 fusion.22
  76.6 0.4 fusion.21
  77.0 0.4 fusion.20
  77.4 0.4 fusion.19
  77.8 0.3 fusion.18
  78.1 0.4 fusion.17
  78.5 0.4 fusion.16
  78.9 0.4 fusion.15
  79.3 0.3 fusion.14
  79.7 0.5 fusion.13
  80.2 0.3 fusion.12
  80.5 0.4 fusion.11
  80.9 0.4 fusion.10
  81.3 0.4 fusion.9
  81.6 0.4 fusion.8
  82.0 0.4 fusion.7
  82.4 0.4 fusion.6
  82.7 0.4 fusion.5
  83.1 0.4 fusion.4
  83.5 0.4 fusion.3
  83.9 0.4 fusion.2
  84.2 0.4 fusion.1
  84.6 1.4 broadcast_multiply_fusion
  86.1 0.2 fusion.70
  86.3 1.3 collective-permute-start.7
  87.6 4.6 %collective-permute-start.6 = (bf16[2,16,8,1,128]{4,3,2,1,0:T(2,128)(2,1)S(1)}, bf16[2,16,8,1,128]{4,3,2,1,0:T(2,128)(2,1)S(1)}, u32[]{:S(2)}, u32[]{:S(2)}) collective-permute-start(bf16[2,16,8,1,128]{4,3,2,1,0:T(2,128)(2,1)S(1)} %get-tuple-element.35), channel_id=1, source_target_pairs={{0,1},{1,2},{2,3},{3,4},{4,5},{5,6},{6,7},{8,9},{9,10},{10,11},{11... | collective-permute-start | bytes 196616 | tf_op jit(solution)/shard_map/ppermute | solution.py:15
  92.2 1.0 collective-permute-done.7
  93.3 1.3 collective-permute-done.6
  95.0 1.3 collective-permute-start.9
  96.3 18.0 %collective-permute-start.8 = (bf16[2,16,1,10,128]{4,3,2,1,0:T(8,128)(2,1)S(1)}, bf16[2,16,1,10,128]{4,3,2,1,0:T(8,128)(2,1)S(1)}, u32[]{:S(2)}, u32[]{:S(2)}) collective-permute-start(bf16[2,16,1,10,128]{4,3,2,1,0:T(8,128)(2,1)S(1)} %get-tuple-element.31), channel_id=1, source_target_pairs={{0,4},{1,5},{2,6},{3,7},{8,12},{9,13},{10,14},{11,15},{16,20},{17,... | collective-permute-start | bytes 245768 | tf_op jit(solution)/shard_map/ppermute | solution.py:15
  114.3 3.2 %collective-permute-done.9 = bf16[2,16,1,10,128]{4,3,2,1,0:T(8,128)(2,1)S(1)} collective-permute-done((bf16[2,16,1,10,128]{4,3,2,1,0:T(8,128)(2,1)S(1)}, bf16[2,16,1,10,128]{4,3,2,1,0:T(8,128)(2,1)S(1)}, u32[]{:S(2)}, u32[]{:S(2)}) %collective-permute-start.9) | collective-permute-done | bytes 81952 | tf_op jit(solution)/shard_map/ppermute | solution.py:15
  117.5 0.3 collective-permute-done.8
  117.9 0.7 collective-permute-start.11
  118.5 0.9 collective-permute-start.10
  119.5 0.7 pad_maximum_fusion.1
  120.2 39.6 %reduce-scatter.2.cloned.1.call-done = f32[432,128]{1,0:T(8,128)} async-done(((f32[3456,128]{1,0:T(8,128)}), f32[432,128]{1,0:T(8,128)}) %reduce-scatter.2.cloned.1.call-update) | async-done | bytes 221200 | tf_op jit(solution)/shard_map/reduce_scatter | solution.py:104
  159.9 7.3 %fusion = bf16[2,1,16,8,8,128]{5,0,4,3,2,1:T(2,128)(2,1)S(1)} fusion(bf16[3,3,3,128,128]{4,3,2,1,0:T(8,128)(2,1)} %bitcast.273, bf16[2,18,10,10,128]{4,3,2,1,0:T(8,128)(2,1)S(1)} %pad_maximum_fusion.1), kind=kOutput, calls=%fused_computation.7 | convolution fusion | flops 1812201472 | bytes 2330624 | tf_op jit(solution)/shard_map/conv_general_dilated | solution.py:19
  167.2 0.9 copy.134
  168.1 24.8 %all-reduce.2.cloned.1.call-done = f32[432,128]{1,0:T(8,128)} async-done(((f32[432,128]{1,0:T(8,128)}), f32[432,128]{1,0:T(8,128)}) %all-reduce.2.cloned.1.call-update) | async-done | bytes 221200 | tf_op jit(solution)/shard_map/psum | solution.py:105
  192.9 1.8 divide_subtract_fusion
  194.8 1.6 copy.256
  (36 shorter events, 1.2 us)
Async XLA Ops:
  7.2 13.0 %copy-start = (bf16[2,1,16,8,8,128]{5,4,3,2,1,0:T(8,128)(2,1)S(1)}, bf16[2,1,16,8,8,128]{5,4,3,2,1,0:T(8,128)(2,1)}, u32[]{:S(2)}) copy-start(bf16[2,1,16,8,8,128]{5,4,3,2,1,0:T(8,128)(2,1)} %param.5) | copy-start | bytes 1572868
  7.2 152.7 %reduce-scatter.2.cloned.1.call-start = ((), (), s32[]{:S(2)}) async-start(), calls=%async_computation.1 | async-start | bytes 1990656 | tf_op jit(solution)/shard_map/reduce_scatter | solution.py:104
  8.7 8.4 %collective-permute-start.1 = (bf16[2,16,8,1,128]{4,3,2,1,0:T(2,128)(2,1)S(1)}, bf16[2,16,8,1,128]{4,3,2,1,0:T(2,128)(2,1)S(1)}, u32[]{:S(2)}, u32[]{:S(2)}) collective-permute-start(bf16[2,16,8,1,128]{4,3,2,1,0:T(2,128)(2,1)S(1)} %get-tuple-element.38), channel_id=1, source_target_pairs={{1,0},{2,1},{3,2},{4,3},{5,4},{6,5},{7,6},{9,8},{10,9},{11,10},{12... | collective-permute-start | bytes 196616 | tf_op jit(solution)/shard_map/ppermute | solution.py:15
  10.0 10.1 %collective-permute-start = (bf16[2,16,8,1,128]{4,3,2,1,0:T(2,128)(2,1)S(1)}, bf16[2,16,8,1,128]{4,3,2,1,0:T(2,128)(2,1)S(1)}, u32[]{:S(2)}, u32[]{:S(2)}) collective-permute-start(bf16[2,16,8,1,128]{4,3,2,1,0:T(2,128)(2,1)S(1)} %get-tuple-element.37), channel_id=1, source_target_pairs={{0,1},{1,2},{2,3},{3,4},{4,5},{5,6},{6,7},{8,9},{9,10},{10,11},{11... | collective-permute-start | bytes 196616 | tf_op jit(solution)/shard_map/ppermute | solution.py:15
  20.4 38.5 %collective-permute-start.3 = (bf16[2,16,1,10,128]{4,3,2,1,0:T(8,128)(2,1)S(1)}, bf16[2,16,1,10,128]{4,3,2,1,0:T(8,128)(2,1)S(1)}, u32[]{:S(2)}, u32[]{:S(2)}) collective-permute-start(bf16[2,16,1,10,128]{4,3,2,1,0:T(8,128)(2,1)S(1)} %get-tuple-element.34), channel_id=1, source_target_pairs={{4,0},{5,1},{6,2},{7,3},{12,8},{13,9},{14,10},{15,11},{20,16},{21,... | collective-permute-start | bytes 245768 | tf_op jit(solution)/shard_map/ppermute | solution.py:15
  57.6 9.0 %copy-start.2 = (bf16[3456,128]{1,0:T(8,128)(2,1)}, bf16[3456,128]{1,0:T(8,128)(2,1)S(1)}, u32[]{:S(2)}) copy-start(bf16[3456,128]{1,0:T(8,128)(2,1)S(1)} %all_gather.3) | copy-start | bytes 2654212
  57.6 3.8 %collective-permute-start.2 = (bf16[2,16,1,10,128]{4,3,2,1,0:T(8,128)(2,1)S(1)}, bf16[2,16,1,10,128]{4,3,2,1,0:T(8,128)(2,1)S(1)}, u32[]{:S(2)}, u32[]{:S(2)}) collective-permute-start(bf16[2,16,1,10,128]{4,3,2,1,0:T(8,128)(2,1)S(1)} %get-tuple-element.33), channel_id=1, source_target_pairs={{0,4},{1,5},{2,6},{3,7},{8,12},{9,13},{10,14},{11,15},{16,20},{17,... | collective-permute-start | bytes 245768 | tf_op jit(solution)/shard_map/ppermute | solution.py:15
  61.5 2.7 %collective-permute-start.5 = (bf16[2,1,10,10,128]{4,3,2,1,0:T(8,128)(2,1)S(1)}, bf16[2,1,10,10,128]{4,3,2,1,0:T(8,128)(2,1)S(1)}, u32[]{:S(2)}, u32[]{:S(2)}) collective-permute-start(bf16[2,1,10,10,128]{4,3,2,1,0:T(8,128)(2,1)S(1)} %get-tuple-element.28), channel_id=1, source_target_pairs={} | collective-permute-start | bytes 153608 | tf_op jit(solution)/shard_map/ppermute | solution.py:15
  63.5 0.7 collective-permute-start.4
  66.5 6.3 %copy-start.3 = (bf16[2,1,16,8,8,128]{5,4,3,2,1,0:T(8,128)(2,1)S(1)}, bf16[2,1,16,8,8,128]{5,4,3,2,1,0:T(8,128)(2,1)}, u32[]{:S(2)}) copy-start(bf16[2,1,16,8,8,128]{5,4,3,2,1,0:T(8,128)(2,1)} %param.9) | copy-start | bytes 1572868
  86.1 106.9 %all-reduce.2.cloned.1.call-start = ((), (), s32[]{:S(2)}) async-start(), calls=%async_computation.2 | async-start | bytes 442368 | tf_op jit(solution)/shard_map/psum | solution.py:105
  86.3 6.9 %collective-permute-start.7 = (bf16[2,16,8,1,128]{4,3,2,1,0:T(2,128)(2,1)S(1)}, bf16[2,16,8,1,128]{4,3,2,1,0:T(2,128)(2,1)S(1)}, u32[]{:S(2)}, u32[]{:S(2)}) collective-permute-start(bf16[2,16,8,1,128]{4,3,2,1,0:T(2,128)(2,1)S(1)} %get-tuple-element.36), channel_id=1, source_target_pairs={{1,0},{2,1},{3,2},{4,3},{5,4},{6,5},{7,6},{9,8},{10,9},{11,10},{12... | collective-permute-start | bytes 196616 | tf_op jit(solution)/shard_map/ppermute | solution.py:15
  87.6 7.1 %collective-permute-start.6 = (bf16[2,16,8,1,128]{4,3,2,1,0:T(2,128)(2,1)S(1)}, bf16[2,16,8,1,128]{4,3,2,1,0:T(2,128)(2,1)S(1)}, u32[]{:S(2)}, u32[]{:S(2)}) collective-permute-start(bf16[2,16,8,1,128]{4,3,2,1,0:T(2,128)(2,1)S(1)} %get-tuple-element.35), channel_id=1, source_target_pairs={{0,1},{1,2},{2,3},{3,4},{4,5},{5,6},{6,7},{8,9},{9,10},{10,11},{11... | collective-permute-start | bytes 196616 | tf_op jit(solution)/shard_map/ppermute | solution.py:15
  95.0 22.5 %collective-permute-start.9 = (bf16[2,16,1,10,128]{4,3,2,1,0:T(8,128)(2,1)S(1)}, bf16[2,16,1,10,128]{4,3,2,1,0:T(8,128)(2,1)S(1)}, u32[]{:S(2)}, u32[]{:S(2)}) collective-permute-start(bf16[2,16,1,10,128]{4,3,2,1,0:T(8,128)(2,1)S(1)} %get-tuple-element.32), channel_id=1, source_target_pairs={{4,0},{5,1},{6,2},{7,3},{12,8},{13,9},{14,10},{15,11},{20,16},{21,... | collective-permute-start | bytes 245768 | tf_op jit(solution)/shard_map/ppermute | solution.py:15
  96.3 21.5 %collective-permute-start.8 = (bf16[2,16,1,10,128]{4,3,2,1,0:T(8,128)(2,1)S(1)}, bf16[2,16,1,10,128]{4,3,2,1,0:T(8,128)(2,1)S(1)}, u32[]{:S(2)}, u32[]{:S(2)}) collective-permute-start(bf16[2,16,1,10,128]{4,3,2,1,0:T(8,128)(2,1)S(1)} %get-tuple-element.31), channel_id=1, source_target_pairs={{0,4},{1,5},{2,6},{3,7},{8,12},{9,13},{10,14},{11,15},{16,20},{17,... | collective-permute-start | bytes 245768 | tf_op jit(solution)/shard_map/ppermute | solution.py:15
  117.9 1.6 collective-permute-start.11
  118.5 0.9 collective-permute-start.10
  159.9 33.1 %copy-start.1 = (f32[432,128]{1,0:T(8,128)S(1)}, f32[432,128]{1,0:T(8,128)}, u32[]{:S(2)}) copy-start(f32[432,128]{1,0:T(8,128)} %param.6) | copy-start | bytes 663556
  159.9 33.1 %copy-start.4 = (f32[432,128]{1,0:T(8,128)S(1)}, f32[432,128]{1,0:T(8,128)}, u32[]{:S(2)}) copy-start(f32[432,128]{1,0:T(8,128)} %param.7) | copy-start | bytes 663556
  159.9 33.1 %copy-start.5 = (f32[432,128]{1,0:T(8,128)S(1)}, f32[432,128]{1,0:T(8,128)}, u32[]{:S(2)}) copy-start(f32[432,128]{1,0:T(8,128)} %param.8) | copy-start | bytes 663556
Sparse Core Ops, SparseCore 0:
  86.2 73.5 reduce-scatter.1
  162.2 30.7 all-reduce.1
where the time goes:
time: 204 us; the launch traced here: 203 us
  waiting for transfers between devices  76.2 us (37%)
  starting transfers between devices  37.5 us (18%)
  blocking collectives  35.9 us (18%)
  matrix products  23.6 us (12%)
  between operations  14.5 us (7%)
  other arithmetic  11.4 us (6%)
  local copies, waits for them, and re-layouts  4.21 us (2%)
    reduce_scatter x1, waiting for transfers between devices, local(): lax.psum_scatter(local_terms, 'space', scatter_dimension=0, tiled=True)  39.6 us
    ppermute x12, starting transfers between devices, shifted(): return lax.ppermute(value, axis, pairs)  37.4 us
    all_gather x1, blocking collectives, local(): whole = lax.all_gather(rows_bf, 'space', axis=0, tiled=True)  35.9 us
    psum x1, waiting for transfers between devices, local(): weight_grad = lax.psum(owned, 'sample')  24.8 us
    conv_general_dilated x2, matrix products, convolve(): lax.conv_general_dilated(field, kernel, (1, 1, 1), 'VALID', dimension_num...  13.5 us
    ppermute x12, waiting for transfers between devices, shifted(): return lax.ppermute(value, axis, pairs)  11.7 us
    dot_general x27, matrix products, kernel_terms(): lax.dot_general(window, grad_pre, (((0, 1, 2, 3), (0, 1, 2, 3)), ((), ())...  10.1 us
    concatenate x4, other arithmetic, extend(): field = jnp.concatenate([below, field, above], dim)  4.4 us
  transfers between devices with their start and end apart: 14, of which 9 were waited for; matrix products, arithmetic and copies ran while one was open for 6% of the time, Pallas kernels for 0%

commit v1 on v0

--- a/solution.py
+++ b/solution.py
@@ -102,7 +102,11 @@
     )
     local_terms = kernel_terms(padded, grad_pre) * float(total) ** (-0.5)
     owned = lax.psum_scatter(local_terms, "space", scatter_dimension=0, tiled=True)
-    weight_grad = lax.psum(owned, "sample")
+    weight_grad = owned
+    for hop in (1, 2):
+        weight_grad = weight_grad + lax.ppermute(
+            weight_grad, "sample", [(dev, dev ^ hop) for dev in range(4)]
+        )
     new_moment = 0.9 * moment + 0.1 * weight_grad
     new_second = 0.999 * second + 0.001 * weight_grad * weight_grad
     first_fix = 1.0 - 0.9**10

time: 204 us -> 179 us (0.88)
  waiting for transfers between devices: 76.2 us -> 53.2 us
    psum x1 -> x0, waiting for transfers between devices: 24.8 us -> none  [local(): weight_grad = lax.psum(owned, 'sample')]
  transfers between devices with their start and end apart: 14 -> 15, of which waited for: 9 -> 9; matrix products, arithmetic and copies ran while one was open for 6% -> 6% of each run, Pallas kernels for 0% -> 0%
where the time goes in v1:
time: 179 us; the launch traced here: 178 us
  waiting for transfers between devices  53.2 us (30%)
  starting transfers between devices  39 us (22%)
  blocking collectives  35.9 us (20%)
  matrix products  22.5 us (13%)
  between operations  14.5 us (8%)
  other arithmetic  10.5 us (6%)
  local copies, waits for them, and re-layouts  2.64 us (1%)
    reduce_scatter x1, waiting for transfers between devices, local(): lax.psum_scatter(local_terms, 'space', scatter_dimension=0, tiled=True)  40.4 us
    ppermute x12, starting transfers between devices, shifted(): return lax.ppermute(value, axis, pairs)  37.4 us
    all_gather x1, blocking collectives, local(): whole = lax.all_gather(rows_bf, 'space', axis=0, tiled=True)  35.9 us
    conv_general_dilated x2, matrix products, convolve(): lax.conv_general_dilated(field, kernel, (1, 1, 1), 'VALID', dimension_num...  12.5 us
    ppermute x12, waiting for transfers between devices, shifted(): return lax.ppermute(value, axis, pairs)  11.9 us
    dot_general x27, matrix products, kernel_terms(): lax.dot_general(window, grad_pre, (((0, 1, 2, 3), (0, 1, 2, 3)), ((), ())...  10.1 us
    concatenate x4, other arithmetic, extend(): field = jnp.concatenate([below, field, above], dim)  4.39 us
  transfers between devices with their start and end apart: 15, of which 9 were waited for; matrix products, arithmetic and copies ran while one was open for 6% of the time, Pallas kernels for 0%

profile of v1, /device:TPU:0, one launch (start us, length us, event | category | flops | bytes accessed | tf_op | source)
XLA Modules:
  0.0 178.3 jit_solution(10320422914187150333)
XLA Ops:
  7.2 1.5 fusion.71
  8.7 1.3 collective-permute-start.1
  10.0 5.5 %collective-permute-start = (bf16[2,16,8,1,128]{4,3,2,1,0:T(2,128)(2,1)S(1)}, bf16[2,16,8,1,128]{4,3,2,1,0:T(2,128)(2,1)S(1)}, u32[]{:S(2)}, u32[]{:S(2)}) collective-permute-start(bf16[2,16,8,1,128]{4,3,2,1,0:T(2,128)(2,1)S(1)} %get-tuple-element.38), channel_id=1, source_target_pairs={{0,1},{1,2},{2,3},{3,4},{4,5},{5,6},{6,7},{8,9},{9,10},{10,11},{11... | collective-permute-start | bytes 196616 | tf_op jit(solution)/shard_map/ppermute | solution.py:15
  15.6 1.0 convert_element_type.18
  16.6 0.6 collective-permute-done.1
  17.3 2.8 %collective-permute-done = bf16[2,16,8,1,128]{4,3,2,1,0:T(2,128)(2,1)S(1)} collective-permute-done((bf16[2,16,8,1,128]{4,3,2,1,0:T(2,128)(2,1)S(1)}, bf16[2,16,8,1,128]{4,3,2,1,0:T(2,128)(2,1)S(1)}, u32[]{:S(2)}, u32[]{:S(2)}) %collective-permute-start) | collective-permute-done | bytes 65568 | tf_op jit(solution)/shard_map/ppermute | solution.py:15
  20.4 1.3 collective-permute-start.3
  21.7 35.9 %all_gather.3 = bf16[3456,128]{1,0:T(8,128)(2,1)S(1)} all-gather(bf16[432,128]{1,0:T(8,128)(2,1)S(1)} %convert_element_type.18), channel_id=1, replica_groups=mesh['sample'=4,'space'=8] {'space'}, dimensions={0}, use_global_device_ids=true | all-gather | bytes 995328 | tf_op jit(solution)/shard_map/all_gather | solution.py:85
  57.6 1.3 collective-permute-start.2
  59.0 2.5 %collective-permute-done.2 = bf16[2,16,1,10,128]{4,3,2,1,0:T(8,128)(2,1)S(1)} collective-permute-done((bf16[2,16,1,10,128]{4,3,2,1,0:T(8,128)(2,1)S(1)}, bf16[2,16,1,10,128]{4,3,2,1,0:T(8,128)(2,1)S(1)}, u32[]{:S(2)}, u32[]{:S(2)}) %collective-permute-start.2) | collective-permute-done | bytes 81952 | tf_op jit(solution)/shard_map/ppermute | solution.py:15
  61.5 0.7 collective-permute-start.5
  62.2 1.4 pad_maximum_fusion.3
  63.6 0.7 collective-permute-start.4
  64.3 0.7 pad_maximum_fusion
  65.0 1.5 pad_maximum_fusion.2
  66.6 6.3 %fusion.36 = f32[2,16,8,8,128]{4,0,3,2,1:T(2,128)S(1)} fusion(bf16[3,3,3,128,128]{4,3,2,1,0:T(8,128)(2,1)S(1)} %bitcast.272, bf16[2,18,10,10,128]{4,3,2,1,0:T(8,128)(2,1)S(1)} %pad_maximum_fusion), kind=kOutput, calls=%fused_computation.73 | convolution fusion | flops 1811939328 | bytes 2854912 | tf_op jit(solution)/shard_map/conv_general_dilated | solution.py:19
  72.9 1.6 fusion.34
  74.5 0.3 fusion.27
  74.8 0.4 fusion.26
  75.2 0.4 fusion.25
  75.6 0.3 fusion.24
  75.9 0.4 fusion.23
  76.3 0.4 fusion.22
  76.7 0.4 fusion.21
  77.0 0.4 fusion.20
  77.4 0.4 fusion.19
  77.8 0.4 fusion.18
  78.2 0.4 fusion.17
  78.5 0.4 fusion.16
  78.9 0.4 fusion.15
  79.4 0.3 fusion.14
  79.7 0.5 fusion.13
  80.2 0.3 fusion.12
  80.6 0.4 fusion.11
  80.9 0.4 fusion.10
  81.3 0.4 fusion.9
  81.7 0.4 fusion.8
  82.1 0.4 fusion.7
  82.4 0.4 fusion.6
  82.8 0.4 fusion.5
  83.2 0.4 fusion.4
  83.6 0.4 fusion.3
  83.9 0.4 fusion.2
  84.3 0.4 fusion.1
  84.7 1.4 broadcast_multiply_fusion
  86.1 0.2 fusion.70
  86.3 1.3 collective-permute-start.7
  87.6 4.6 %collective-permute-start.6 = (bf16[2,16,8,1,128]{4,3,2,1,0:T(2,128)(2,1)S(1)}, bf16[2,16,8,1,128]{4,3,2,1,0:T(2,128)(2,1)S(1)}, u32[]{:S(2)}, u32[]{:S(2)}) collective-permute-start(bf16[2,16,8,1,128]{4,3,2,1,0:T(2,128)(2,1)S(1)} %get-tuple-element.36), channel_id=1, source_target_pairs={{0,1},{1,2},{2,3},{3,4},{4,5},{5,6},{6,7},{8,9},{9,10},{10,11},{11... | collective-permute-start | bytes 196616 | tf_op jit(solution)/shard_map/ppermute | solution.py:15
  92.2 1.0 collective-permute-done.7
  93.3 1.3 collective-permute-done.6
  94.8 0.2 pad_maximum_fusion.10
  95.0 1.3 collective-permute-start.9
  96.3 18.0 %collective-permute-start.8 = (bf16[2,16,1,10,128]{4,3,2,1,0:T(8,128)(2,1)S(1)}, bf16[2,16,1,10,128]{4,3,2,1,0:T(8,128)(2,1)S(1)}, u32[]{:S(2)}, u32[]{:S(2)}) collective-permute-start(bf16[2,16,1,10,128]{4,3,2,1,0:T(8,128)(2,1)S(1)} %get-tuple-element.32), channel_id=1, source_target_pairs={{0,4},{1,5},{2,6},{3,7},{8,12},{9,13},{10,14},{11,15},{16,20},{17,... | collective-permute-start | bytes 245768 | tf_op jit(solution)/shard_map/ppermute | solution.py:15
  114.2 3.3 %collective-permute-done.9 = bf16[2,16,1,10,128]{4,3,2,1,0:T(8,128)(2,1)S(1)} collective-permute-done((bf16[2,16,1,10,128]{4,3,2,1,0:T(8,128)(2,1)S(1)}, bf16[2,16,1,10,128]{4,3,2,1,0:T(8,128)(2,1)S(1)}, u32[]{:S(2)}, u32[]{:S(2)}) %collective-permute-start.9) | collective-permute-done | bytes 81952 | tf_op jit(solution)/shard_map/ppermute | solution.py:15
  117.6 0.3 collective-permute-done.8
  118.0 0.7 collective-permute-start.11
  118.7 0.9 collective-permute-start.10
  119.7 40.4 %reduce-scatter.2.cloned.1.call-done = f32[432,128]{1,0:T(8,128)} async-done(((f32[3456,128]{1,0:T(8,128)}), f32[432,128]{1,0:T(8,128)}) %reduce-scatter.2.cloned.1.call-update) | async-done | bytes 221200 | tf_op jit(solution)/shard_map/reduce_scatter | solution.py:104
  160.0 0.7 pad_maximum_fusion.1
  160.8 0.9 collective-permute-done.12
  161.8 1.6 collective-permute-start.13
  163.4 6.2 %fusion = bf16[2,1,16,8,8,128]{5,0,4,3,2,1:T(2,128)(2,1)S(1)} fusion(bf16[3,3,3,128,128]{4,3,2,1,0:T(8,128)(2,1)S(1)} %bitcast.273, bf16[2,18,10,10,128]{4,3,2,1,0:T(8,128)(2,1)S(1)} %pad_maximum_fusion.1), kind=kOutput, calls=%fused_computation.7 | convolution fusion | flops 1812201472 | bytes 2330624 | tf_op jit(solution)/shard_map/conv_general_dilated | solution.py:19
  169.6 0.9 copy.134
  170.5 1.0 divide_subtract_fusion
  (37 shorter events, 1.1 us)
Async XLA Ops:
  7.2 13.1 %copy-start = (bf16[2,1,16,8,8,128]{5,4,3,2,1,0:T(8,128)(2,1)S(1)}, bf16[2,1,16,8,8,128]{5,4,3,2,1,0:T(8,128)(2,1)}, u32[]{:S(2)}) copy-start(bf16[2,1,16,8,8,128]{5,4,3,2,1,0:T(8,128)(2,1)} %param.5) | copy-start | bytes 1572868
  7.2 152.8 %reduce-scatter.2.cloned.1.call-start = ((), (), s32[]{:S(2)}) async-start(), calls=%async_computation.1 | async-start | bytes 1990656 | tf_op jit(solution)/shard_map/reduce_scatter | solution.py:104
  8.7 8.4 %collective-permute-start.1 = (bf16[2,16,8,1,128]{4,3,2,1,0:T(2,128)(2,1)S(1)}, bf16[2,16,8,1,128]{4,3,2,1,0:T(2,128)(2,1)S(1)}, u32[]{:S(2)}, u32[]{:S(2)}) collective-permute-start(bf16[2,16,8,1,128]{4,3,2,1,0:T(2,128)(2,1)S(1)} %get-tuple-element.39), channel_id=1, source_target_pairs={{1,0},{2,1},{3,2},{4,3},{5,4},{6,5},{7,6},{9,8},{10,9},{11,10},{12... | collective-permute-start | bytes 196616 | tf_op jit(solution)/shard_map/ppermute | solution.py:15
  10.0 10.1 %collective-permute-start = (bf16[2,16,8,1,128]{4,3,2,1,0:T(2,128)(2,1)S(1)}, bf16[2,16,8,1,128]{4,3,2,1,0:T(2,128)(2,1)S(1)}, u32[]{:S(2)}, u32[]{:S(2)}) collective-permute-start(bf16[2,16,8,1,128]{4,3,2,1,0:T(2,128)(2,1)S(1)} %get-tuple-element.38), channel_id=1, source_target_pairs={{0,1},{1,2},{2,3},{3,4},{4,5},{5,6},{6,7},{8,9},{9,10},{10,11},{11... | collective-permute-start | bytes 196616 | tf_op jit(solution)/shard_map/ppermute | solution.py:15
  20.4 38.5 %collective-permute-start.3 = (bf16[2,16,1,10,128]{4,3,2,1,0:T(8,128)(2,1)S(1)}, bf16[2,16,1,10,128]{4,3,2,1,0:T(8,128)(2,1)S(1)}, u32[]{:S(2)}, u32[]{:S(2)}) collective-permute-start(bf16[2,16,1,10,128]{4,3,2,1,0:T(8,128)(2,1)S(1)} %get-tuple-element.35), channel_id=1, source_target_pairs={{4,0},{5,1},{6,2},{7,3},{12,8},{13,9},{14,10},{15,11},{20,16},{21,... | collective-permute-start | bytes 245768 | tf_op jit(solution)/shard_map/ppermute | solution.py:15
  57.6 3.8 %collective-permute-start.2 = (bf16[2,16,1,10,128]{4,3,2,1,0:T(8,128)(2,1)S(1)}, bf16[2,16,1,10,128]{4,3,2,1,0:T(8,128)(2,1)S(1)}, u32[]{:S(2)}, u32[]{:S(2)}) collective-permute-start(bf16[2,16,1,10,128]{4,3,2,1,0:T(8,128)(2,1)S(1)} %get-tuple-element.34), channel_id=1, source_target_pairs={{0,4},{1,5},{2,6},{3,7},{8,12},{9,13},{10,14},{11,15},{16,20},{17,... | collective-permute-start | bytes 245768 | tf_op jit(solution)/shard_map/ppermute | solution.py:15
  61.5 2.7 %collective-permute-start.5 = (bf16[2,1,10,10,128]{4,3,2,1,0:T(8,128)(2,1)S(1)}, bf16[2,1,10,10,128]{4,3,2,1,0:T(8,128)(2,1)S(1)}, u32[]{:S(2)}, u32[]{:S(2)}) collective-permute-start(bf16[2,1,10,10,128]{4,3,2,1,0:T(8,128)(2,1)S(1)} %get-tuple-element.29), channel_id=1, source_target_pairs={} | collective-permute-start | bytes 153608 | tf_op jit(solution)/shard_map/ppermute | solution.py:15
  63.6 0.7 collective-permute-start.4
  66.6 6.3 %copy-start.2 = (bf16[2,1,16,8,8,128]{5,4,3,2,1,0:T(8,128)(2,1)S(1)}, bf16[2,1,16,8,8,128]{5,4,3,2,1,0:T(8,128)(2,1)}, u32[]{:S(2)}) copy-start(bf16[2,1,16,8,8,128]{5,4,3,2,1,0:T(8,128)(2,1)} %param.9) | copy-start | bytes 1572868
  86.3 6.9 %collective-permute-start.7 = (bf16[2,16,8,1,128]{4,3,2,1,0:T(2,128)(2,1)S(1)}, bf16[2,16,8,1,128]{4,3,2,1,0:T(2,128)(2,1)S(1)}, u32[]{:S(2)}, u32[]{:S(2)}) collective-permute-start(bf16[2,16,8,1,128]{4,3,2,1,0:T(2,128)(2,1)S(1)} %get-tuple-element.37), channel_id=1, source_target_pairs={{1,0},{2,1},{3,2},{4,3},{5,4},{6,5},{7,6},{9,8},{10,9},{11,10},{12... | collective-permute-start | bytes 196616 | tf_op jit(solution)/shard_map/ppermute | solution.py:15
  87.6 7.1 %collective-permute-start.6 = (bf16[2,16,8,1,128]{4,3,2,1,0:T(2,128)(2,1)S(1)}, bf16[2,16,8,1,128]{4,3,2,1,0:T(2,128)(2,1)S(1)}, u32[]{:S(2)}, u32[]{:S(2)}) collective-permute-start(bf16[2,16,8,1,128]{4,3,2,1,0:T(2,128)(2,1)S(1)} %get-tuple-element.36), channel_id=1, source_target_pairs={{0,1},{1,2},{2,3},{3,4},{4,5},{5,6},{6,7},{8,9},{9,10},{10,11},{11... | collective-permute-start | bytes 196616 | tf_op jit(solution)/shard_map/ppermute | solution.py:15
  95.0 22.6 %collective-permute-start.9 = (bf16[2,16,1,10,128]{4,3,2,1,0:T(8,128)(2,1)S(1)}, bf16[2,16,1,10,128]{4,3,2,1,0:T(8,128)(2,1)S(1)}, u32[]{:S(2)}, u32[]{:S(2)}) collective-permute-start(bf16[2,16,1,10,128]{4,3,2,1,0:T(8,128)(2,1)S(1)} %get-tuple-element.33), channel_id=1, source_target_pairs={{4,0},{5,1},{6,2},{7,3},{12,8},{13,9},{14,10},{15,11},{20,16},{21,... | collective-permute-start | bytes 245768 | tf_op jit(solution)/shard_map/ppermute | solution.py:15
  96.3 21.7 %collective-permute-start.8 = (bf16[2,16,1,10,128]{4,3,2,1,0:T(8,128)(2,1)S(1)}, bf16[2,16,1,10,128]{4,3,2,1,0:T(8,128)(2,1)S(1)}, u32[]{:S(2)}, u32[]{:S(2)}) collective-permute-start(bf16[2,16,1,10,128]{4,3,2,1,0:T(8,128)(2,1)S(1)} %get-tuple-element.32), channel_id=1, source_target_pairs={{0,4},{1,5},{2,6},{3,7},{8,12},{9,13},{10,14},{11,15},{16,20},{17,... | collective-permute-start | bytes 245768 | tf_op jit(solution)/shard_map/ppermute | solution.py:15
  118.0 1.6 collective-permute-start.11
  118.7 0.9 collective-permute-start.10
  160.0 1.7 copy-start.3
  160.0 1.7 collective-permute-start.12
  161.7 8.8 %copy-start.1 = (f32[432,128]{1,0:T(8,128)S(1)}, f32[432,128]{1,0:T(8,128)}, u32[]{:S(2)}) copy-start(f32[432,128]{1,0:T(8,128)} %param.6) | copy-start | bytes 663556
  161.8 8.8 %copy-start.4 = (f32[432,128]{1,0:T(8,128)S(1)}, f32[432,128]{1,0:T(8,128)}, u32[]{:S(2)}) copy-start(f32[432,128]{1,0:T(8,128)} %param.7) | copy-start | bytes 663556
  161.8 8.8 %copy-start.5 = (f32[432,128]{1,0:T(8,128)S(1)}, f32[432,128]{1,0:T(8,128)}, u32[]{:S(2)}) copy-start(f32[432,128]{1,0:T(8,128)} %param.8) | copy-start | bytes 663556
  161.8 8.7 %collective-permute-start.13 = (f32[432,128]{1,0:T(8,128)S(1)}, f32[432,128]{1,0:T(8,128)S(1)}, u32[]{:S(2)}, u32[]{:S(2)}) collective-permute-start(f32[432,128]{1,0:T(8,128)S(1)} %add.50), channel_id=1, source_target_pairs={{0,16},{8,24},{16,0},{24,8},{1,17},{9,25},{17,1},{25,9},{2,18},{10... | collective-permute-start | bytes 663560 | tf_op jit(solution)/shard_map/ppermute | solution.py:107
Sparse Core Ops, SparseCore 0:
  86.3 73.7 reduce-scatter.1
